TPU v7x, 256 devices: a whole 4x4x8 slice. The times are simulated.
256 devices in a mesh: section: 8 (over y, core), ctx: 32 (over z, x).
Axes of the slice: x: 4, y: 4, z: 8, core: 2. Of those that a mesh axis runs over, the one named last changes fastest.
Arguments:
- section_input: bfloat16 [2, 4096, 2048], P(None, 'ctx'), may hold values from -6 to 6
- cotangent: bfloat16 [2, 4096, 2048], P(None, 'ctx'), may hold values from -6 to 6
- w_query: bfloat16 [8, 2048, 1024], P('section', 'ctx'), may hold values from -0.125 to 0.125
- w_key: bfloat16 [8, 2048, 1024], P('section', 'ctx'), may hold values from -0.125 to 0.125
- w_value: bfloat16 [8, 2048, 1024], P('section', 'ctx'), may hold values from -0.125 to 0.125
- w_out: bfloat16 [8, 1024, 2048], P('section', 'ctx'), may hold values from -0.1875 to 0.1875
- block_mask: int32 [2, 128, 2], P(None, 'ctx'), may hold values 0 or 1
Outputs:
- section_output: bfloat16 [8, 2, 4096, 2048], P('section', None, 'ctx')
- input_grad: bfloat16 [8, 2, 4096, 2048], P('section', None, 'ctx')
Inputs may be any that keep to these rules, and one draw needn't show every extreme that they name: A block always attends to itself; column 0 and 1 of block_mask choose its two neighbour blocks.
All inputs are finite; a program needn't handle non-finite values.
Results may differ from a plain program's by a relative error of at most 0.03.
Values may be sent and summed in bfloat16 or wider, within the bound.
No kernel may reach another device: no remote copies, remote signals or barrier semaphores. Data moves between devices by JAX's collectives and lax.ppermute only.
A program may use at most 128 MiB of HBM per device.

v0:
```python
import jax
import jax.numpy as jnp
from jax import lax
from jax.sharding import PartitionSpec as P

D = 2048
HEADS = 8
HDIM = 128
BLOCKS_DEV = 4
BLK = 32


def padded(block, sides, width):
    for axis, dim in sides:
        count = lax.axis_size(axis)
        forward = [(i, i + 1) for i in range(count - 1)]
        backward = [(target, source) for source, target in forward]
        low = lax.ppermute(
            lax.slice_in_dim(block, block.shape[dim] - width, None, axis=dim), axis, forward
        )
        high = lax.ppermute(lax.slice_in_dim(block, 0, width, axis=dim), axis, backward)
        block = jnp.concatenate([low, block, high], axis=dim)
    return block


def shifted(block, axis, distance):
    devices = range(lax.axis_size(axis))
    route = [(i - distance, i) for i in devices if i - distance in devices]
    return lax.ppermute(block, axis, route)


def rms_scale(values):
    return values * lax.rsqrt(jnp.mean(values * values, axis=-1, keepdims=True) + 1e-06)


def allowed_keys(mask_rows, block_ids, block_count):
    mask_float = mask_rows.astype(jnp.float32)
    left = mask_float[:, 0] * (block_ids > 0).astype(jnp.float32)
    right = mask_float[:, 1] * (block_ids < block_count - 1).astype(jnp.float32)
    return jnp.stack([left, jnp.ones_like(left), right], axis=1)


def project(layer_in, w_query, w_key, w_value):
    length = layer_in.shape[0]
    normed = rms_scale(layer_in.astype(jnp.float32)).astype(jnp.bfloat16)

    def head_normed(weight):
        out = jnp.dot(normed, weight, preferred_element_type=jnp.float32)
        out = rms_scale(out.reshape(length, HEADS, HDIM))
        return out.reshape(length, HEADS * HDIM).astype(jnp.bfloat16)

    query = head_normed(w_query)
    key = head_normed(w_key)
    value = jnp.dot(normed, w_value, preferred_element_type=jnp.float32).astype(jnp.bfloat16)
    return (query, key, value)


def attend(query, keys_ext, values_ext, allow, layer_in, w_out):
    length = query.shape[0]
    nblock = length // BLK
    queries = query.reshape(nblock, BLK, HEADS, HDIM)

    def windows(extended):
        grid = extended.reshape(nblock + 2, BLK, HEADS, HDIM)
        return jnp.concatenate([grid[:-2], grid[1:-1], grid[2:]], axis=1)

    keys = windows(keys_ext)
    values = windows(values_ext)
    scores = jnp.einsum(
        "bqhd,bkhd->bhqk", queries, keys, preferred_element_type=jnp.float32
    ) * HDIM ** (-0.5)
    weight = jnp.repeat(allow, BLK, axis=1)[:, None, None, :]
    probs = jnp.exp(scores) * weight
    total = jnp.sum(probs, axis=-1)
    attended = jnp.einsum(
        "bhqk,bkhd->bqhd", probs.astype(jnp.bfloat16), values, preferred_element_type=jnp.float32
    )
    attended = attended / jnp.transpose(total, (0, 2, 1))[..., None]
    attended = attended.reshape(length, HEADS * HDIM).astype(jnp.bfloat16)
    update = jnp.dot(attended, w_out, preferred_element_type=jnp.float32)
    return (layer_in.astype(jnp.float32) + update).astype(jnp.bfloat16)


def put_slot(buffer, value, slot, active):
    return jnp.where(active, lax.dynamic_update_index_in_dim(buffer, value, slot, 0), buffer)


def take_slot(buffer, slot):
    return lax.dynamic_index_in_dim(buffer, slot, 0, keepdims=False)


def per_device(section_input, cotangent, w_query, w_key, w_value, w_out, block_mask):
    n_section = lax.axis_size("section")
    n_ctx = lax.axis_size("ctx")
    section = lax.axis_index("section")
    place = lax.axis_index("ctx")
    micro = section_input.shape[0]
    length = section_input.shape[1]
    width = HEADS * HDIM
    full_query, full_key, full_value, full_out = (
        lax.all_gather(w_query[0], "ctx", axis=0, tiled=True),
        lax.all_gather(w_key[0], "ctx", axis=0, tiled=True),
        lax.all_gather(w_value[0], "ctx", axis=0, tiled=True),
        lax.all_gather(w_out[0], "ctx", axis=0, tiled=True),
    )
    block_ids = place * BLOCKS_DEV + jnp.arange(BLOCKS_DEV)
    allows = jax.vmap(lambda rows_mask: allowed_keys(rows_mask, block_ids, BLOCKS_DEV * n_ctx))(
        block_mask
    )
    zero_rows = jnp.zeros((length, D), jnp.bfloat16)
    zero_heads = jnp.zeros((length, width), jnp.bfloat16)
    zero_wide = jnp.zeros((length + 2 * BLK, width), jnp.bfloat16)
    steps_total = n_section + micro - 1

    def run_project(values):
        return project(values, full_query, full_key, full_value)

    def skip_project(values):
        return (zero_heads, zero_heads, zero_heads)

    def run_attend(query, extended, layer_in, allow):
        return attend(query, extended[0], extended[1], allow, layer_in, full_out)

    def skip_attend(query, extended, layer_in, allow):
        return zero_rows

    kv_store = jnp.zeros((micro, 2, length, width), jnp.bfloat16)
    inputs = jnp.zeros((micro, length, D), jnp.bfloat16)
    outputs = jnp.zeros((micro, length, D), jnp.bfloat16)
    queries = jnp.zeros((micro, length, width), jnp.bfloat16)

    def forward_step(step, carry):
        incoming, inputs, outputs, queries, kv_store = carry
        micro_id = step - section
        active = (micro_id >= 0) & (micro_id < micro)
        slot = jnp.clip(micro_id, 0, micro - 1)
        layer_in = jnp.where(section == 0, take_slot(section_input, slot), incoming)
        query, key, value = lax.cond(active, run_project, skip_project, layer_in)
        local_kv = jnp.stack([key, value])
        extended = padded(local_kv, (("ctx", 1),), BLK)
        allow = take_slot(allows, slot)
        result = lax.cond(active, run_attend, skip_attend, query, extended, layer_in, allow)
        inputs = put_slot(inputs, layer_in, slot, active)
        outputs = put_slot(outputs, result, slot, active)
        queries = put_slot(queries, query, slot, active)
        kv_store = put_slot(kv_store, local_kv, slot, active)
        incoming = shifted(result, "section", 1)
        return (incoming, inputs, outputs, queries, kv_store)

    carry = (zero_rows, inputs, outputs, queries, kv_store)
    _, inputs, outputs, queries, kv_store = lax.fori_loop(0, steps_total, forward_step, carry)

    def pull_attend(query, extended, layer_in, allow, grad_in):

        def local_attend(query_in, keys_in, values_in, rows_in):
            return attend(query_in, keys_in, values_in, allow, rows_in, full_out)

        _, pull = jax.vjp(local_attend, query, extended[0], extended[1], layer_in)
        return pull(grad_in)

    def skip_pull(query, extended, layer_in, allow, grad_in):
        return (zero_heads, zero_wide, zero_wide, zero_rows)

    def pull_project(layer_in, d_query, own):
        _, pull = jax.vjp(run_project, layer_in)
        return pull((d_query, own[0], own[1]))[0]

    def skip_pull_project(layer_in, d_query, own):
        return zero_rows

    grads = jnp.zeros((micro, length, D), jnp.bfloat16)

    def backward_step(step, carry):
        incoming, grads = carry
        micro_id = step - (n_section - 1 - section)
        active = (micro_id >= 0) & (micro_id < micro)
        slot = jnp.clip(micro_id, 0, micro - 1)
        grad_in = jnp.where(section == n_section - 1, take_slot(cotangent, slot), incoming)
        layer_in = take_slot(inputs, slot)
        query = take_slot(queries, slot)
        extended = padded(take_slot(kv_store, slot), (("ctx", 1),), BLK)
        allow = take_slot(allows, slot)
        d_query, d_keys, d_values, d_direct = lax.cond(
            active, pull_attend, skip_pull, query, extended, layer_in, allow, grad_in
        )
        d_wide = jnp.stack([d_keys, d_values])
        rims = jnp.concatenate([d_wide[:, :BLK], d_wide[:, -BLK:]], axis=1)
        returned = padded(rims, (("ctx", 1),), BLK)
        own = d_wide[:, BLK:-BLK]
        own = own.at[:, :BLK].add(returned[:, :BLK])
        own = own.at[:, -BLK:].add(returned[:, -BLK:])
        d_projected = lax.cond(active, pull_project, skip_pull_project, layer_in, d_query, own)
        d_input = d_direct + d_projected
        grads = put_slot(grads, d_input, slot, active)
        incoming = shifted(d_input, "section", -1)
        return (incoming, grads)

    _, grads = lax.fori_loop(0, steps_total, backward_step, (zero_rows, grads))
    return (outputs[None], grads[None])


def solution(mesh):
    return jax.shard_map(
        per_device,
        mesh=mesh,
        in_specs=(
            P(None, "ctx", None),
            P(None, "ctx", None),
            P("section", "ctx", None),
            P("section", "ctx", None),
            P("section", "ctx", None),
            P("section", "ctx", None),
            P(None, "ctx", None),
        ),
        out_specs=(P("section", None, "ctx", None), P("section", None, "ctx", None)),
        check_vma=False,
    )
```

profile of v0, /device:TPU:103, one launch (start us, length us, event | category | flops | bytes accessed | tf_op | source)
XLA Modules:
  0.0 1315.3 jit_solution(2852460559565105699)
XLA Ops:
  11.0 78.0 %all-gather.9.cloned.1.call-done = bf16[1,2048,1024]{2,1,0:T(8,128)(2,1)} async-done(((bf16[1,64,1024]{2,1,0:T(8,128)(2,1)}), bf16[1,2048,1024]{2,1,0:T(8,128)(2,1)}) %all-gather.9.cloned.1.call-update) | async-done | bytes 4194320 | tf_op jit(solution)/shard_map/all_gather | solution.py:101
  88.9 81.8 %all-gather.11.cloned.1.call-done = bf16[1,2048,1024]{2,1,0:T(8,128)(2,1)} async-done(((bf16[1,64,1024]{2,1,0:T(8,128)(2,1)}), bf16[1,2048,1024]{2,1,0:T(8,128)(2,1)}) %all-gather.11.cloned.1.call-update) | async-done | bytes 4194320 | tf_op jit(solution)/shard_map/all_gather | solution.py:102
  170.7 81.8 %all-gather.13.cloned.1.call-done = bf16[1,2048,1024]{2,1,0:T(8,128)(2,1)} async-done(((bf16[1,64,1024]{2,1,0:T(8,128)(2,1)}), bf16[1,2048,1024]{2,1,0:T(8,128)(2,1)}) %all-gather.13.cloned.1.call-update) | async-done | bytes 4194320 | tf_op jit(solution)/shard_map/all_gather | solution.py:103
  252.5 81.6 %all-gather.15.cloned.1.call-done = bf16[1,1024,2048]{2,1,0:T(8,128)(2,1)} async-done(((bf16[1,32,2048]{2,1,0:T(8,128)(2,1)}), bf16[1,1024,2048]{2,1,0:T(8,128)(2,1)}) %all-gather.15.cloned.1.call-update) | async-done | bytes 4194320 | tf_op jit(solution)/shard_map/all_gather | solution.py:104
  337.4 301.7 %while.41 = (s32[]{:T(128)}, bf16[128,2048]{1,0:T(8,128)(2,1)S(1)}, bf16[2,128,2048]{2,1,0:T(8,128)(2,1)S(1)}, bf16[2,128,2048]{2,1,0:T(8,128)(2,1)}, bf16[2,128...) while((s32[]{:T(128)}, bf16[128,2048]{1,0:T(8,128)(2,1)S(1)}, ...), condition=%wide.region_9.10_spmd, body=%wide.region_0.9_spmd.sunk | while | flops 2211841024 | bytes 75189416 | solution.py:151
  350.6 7.9 collective-permute-start.2
  362.1 12.5 collective-permute-done.2
  376.0 10.8 conditional.8
  388.8 7.4 collective-permute-start.1
  414.6 10.8 conditional.8
  458.0 7.4 collective-permute-start.1
  468.4 21.3 %collective-permute-start.2 = (bf16[128,2048]{1,0:T(8,128)(2,1)}, bf16[128,2048]{1,0:T(8,128)(2,1)S(1)}, u32[]{:S(2)}, u32[]{:S(2)}) collective-permute-start(bf16[128,2048]{1,0:T(8,128)(2,1)} %get-tuple-element.1251), channel_id=1, source_target_pairs={{0,32},{32,64},{64,96},{96,128},{128,160},{160,192},{192,224},{1,3... | collective-permute-start | bytes 1572872 | tf_op jit(solution)/shard_map/while/body/eval_jaxpr/ppermute | solution.py:29
  499.6 7.4 collective-permute-start.1
  525.0 7.4 collective-permute-start.1
  535.4 8.4 collective-permute-start.2
  553.7 7.4 collective-permute-start.1
  579.1 7.4 collective-permute-start.1
  589.5 17.8 %collective-permute-start.2 = (bf16[128,2048]{1,0:T(8,128)(2,1)}, bf16[128,2048]{1,0:T(8,128)(2,1)S(1)}, u32[]{:S(2)}, u32[]{:S(2)}) collective-permute-start(bf16[128,2048]{1,0:T(8,128)(2,1)} %get-tuple-element.1251), channel_id=1, source_target_pairs={{0,32},{32,64},{64,96},{96,128},{128,160},{160,192},{192,224},{1,3... | collective-permute-start | bytes 1572872 | tf_op jit(solution)/shard_map/while/body/eval_jaxpr/ppermute | solution.py:29
  617.2 7.4 collective-permute-start.1
  641.0 667.8 %while.42 = (s32[]{:T(128)}, bf16[128,2048]{1,0:T(8,128)(2,1)}, bf16[2,128,2048]{2,1,0:T(8,128)(2,1)}, s32[]{:T(128)}, bf16[2,2,128,1024]{3,2,1,0:T(8,128)(2,1)}...) while((s32[]{:T(128)}, bf16[128,2048]{1,0:T(8,128)(2,1)}, ...), condition=%wide.region_24.25_spmd, body=%wide.region_10.24_spmd.sunk | while | flops 3389073152 | bytes 170649296 | solution.py:198
  644.1 7.4 collective-permute-start.4
  655.5 7.1 collective-permute-start.5
  664.5 7.1 collective-permute-done.6
  675.7 15.2 %collective-permute-done.7 = bf16[128,2048]{1,0:T(8,128)(2,1)S(1)} collective-permute-done((bf16[128,2048]{1,0:T(8,128)(2,1)S(1)}, bf16[128,2048]{1,0:T(8,128)(2,1)S(1)}, u32[]{:S(2)}, u32[]{:S(2)}) %collective-permute-start.7) | collective-permute-done | bytes 524320 | tf_op jit(solution)/shard_map/while/body/eval_jaxpr/ppermute | solution.py:29
  706.5 7.1 collective-permute-start.5
  715.6 7.1 collective-permute-done.6
  726.8 9.4 collective-permute-done.7
  750.7 7.1 collective-permute-start.5
  759.8 7.1 collective-permute-done.6
  771.0 22.7 %collective-permute-done.7 = bf16[128,2048]{1,0:T(8,128)(2,1)S(1)} collective-permute-done((bf16[128,2048]{1,0:T(8,128)(2,1)S(1)}, bf16[128,2048]{1,0:T(8,128)(2,1)S(1)}, u32[]{:S(2)}, u32[]{:S(2)}) %collective-permute-start.7) | collective-permute-done | bytes 524320 | tf_op jit(solution)/shard_map/while/body/eval_jaxpr/ppermute | solution.py:29
  808.2 7.1 collective-permute-start.5
  828.4 9.2 collective-permute-done.7
  852.2 7.1 collective-permute-start.5
  861.2 7.1 collective-permute-done.6
  872.5 14.1 %collective-permute-done.7 = bf16[128,2048]{1,0:T(8,128)(2,1)S(1)} collective-permute-done((bf16[128,2048]{1,0:T(8,128)(2,1)S(1)}, bf16[128,2048]{1,0:T(8,128)(2,1)S(1)}, u32[]{:S(2)}, u32[]{:S(2)}) %collective-permute-start.7) | collective-permute-done | bytes 524320 | tf_op jit(solution)/shard_map/while/body/eval_jaxpr/ppermute | solution.py:29
  901.7 7.4 collective-permute-start.5
  911.0 7.1 collective-permute-done.6
  922.3 176.7 %collective-permute-done.7 = bf16[128,2048]{1,0:T(8,128)(2,1)S(1)} collective-permute-done((bf16[128,2048]{1,0:T(8,128)(2,1)S(1)}, bf16[128,2048]{1,0:T(8,128)(2,1)S(1)}, u32[]{:S(2)}, u32[]{:S(2)}) %collective-permute-start.7) | collective-permute-done | bytes 524320 | tf_op jit(solution)/shard_map/while/body/eval_jaxpr/ppermute | solution.py:29
  1111.5 11.2 conditional.10
  1124.6 7.1 collective-permute-start.5
  1140.7 18.6 %conditional.11 = (bf16[128,2048]{1,0:T(8,128)(2,1)S(1)}) conditional(s32[]{:T(128)} %convert_element_type.302, () %tuple.209, (bf16[2,192,1024]{2,1,0:T(8,128)(2,1)S(1)}, bf16[2,32,1024]{2,1,0:T(8,128)(2,1)S(1)}, bf16[2,32,1024]{2,1,0:T(8,128)(2,1)S(1)}, bf16[2048,1024]{1,0:T(8,128)(2,1)}, bf16[2,128,2048]{2,1,0:T(8,128)(2,1)S(1)}, ...), branch_computations={%region_15.15_spmd, %region_16.23_spmd} | conditional | flops 2693800704 | bytes 90314520 | solution.py:192
  1163.4 9.5 collective-permute-done.7
  1185.4 11.2 conditional.10
  1198.5 7.1 collective-permute-start.5
  1214.6 18.6 %conditional.11 = (bf16[128,2048]{1,0:T(8,128)(2,1)S(1)}) conditional(s32[]{:T(128)} %convert_element_type.302, () %tuple.209, (bf16[2,192,1024]{2,1,0:T(8,128)(2,1)S(1)}, bf16[2,32,1024]{2,1,0:T(8,128)(2,1)S(1)}, bf16[2,32,1024]{2,1,0:T(8,128)(2,1)S(1)}, bf16[2048,1024]{1,0:T(8,128)(2,1)}, bf16[2,128,2048]{2,1,0:T(8,128)(2,1)S(1)}, ...), branch_computations={%region_15.15_spmd, %region_16.23_spmd} | conditional | flops 2693800704 | bytes 90314520 | solution.py:192
  1237.4 8.6 collective-permute-done.7
  1260.4 7.1 collective-permute-start.5
  1278.8 27.7 %collective-permute-start.7 = (bf16[128,2048]{1,0:T(8,128)(2,1)S(1)}, bf16[128,2048]{1,0:T(8,128)(2,1)S(1)}, u32[]{:S(2)}, u32[]{:S(2)}) collective-permute-start(bf16[128,2048]{1,0:T(8,128)(2,1)S(1)} %get-tuple-element.1276), channel_id=1, source_target_pairs={{32,0},{64,32},{96,64},{128,96},{160,128},{192,160},{224,192},{33,... | collective-permute-start | bytes 1572872 | tf_op jit(solution)/shard_map/while/body/eval_jaxpr/ppermute | solution.py:29
  (696 shorter events, 476.1 us)
Async XLA Ops:
  7.2 81.8 %all-gather.9.cloned.1.call-start = ((), (), s32[]{:S(2)}) async-start(), calls=%async_computation | async-start | bytes 4325376 | tf_op jit(solution)/shard_map/all_gather | solution.py:101
  7.9 162.8 %all-gather.11.cloned.1.call-start = ((), (), s32[]{:S(2)}) async-start(), calls=%async_computation.1 | async-start | bytes 4325376 | tf_op jit(solution)/shard_map/all_gather | solution.py:102
  8.6 243.8 %all-gather.13.cloned.1.call-start = ((), (), s32[]{:S(2)}) async-start(), calls=%async_computation.2 | async-start | bytes 4325376 | tf_op jit(solution)/shard_map/all_gather | solution.py:103
  9.4 324.7 %all-gather.15.cloned.1.call-start = ((), (), s32[]{:S(2)}) async-start(), calls=%async_computation.3 | async-start | bytes 4325376 | tf_op jit(solution)/shard_map/all_gather | solution.py:104
  338.9 10.7 collective-permute-start
  350.6 24.1 %collective-permute-start.2 = (bf16[128,2048]{1,0:T(8,128)(2,1)}, bf16[128,2048]{1,0:T(8,128)(2,1)S(1)}, u32[]{:S(2)}, u32[]{:S(2)}) collective-permute-start(bf16[128,2048]{1,0:T(8,128)(2,1)} %get-tuple-element.1251), channel_id=1, source_target_pairs={{0,32},{32,64},{64,96},{96,128},{128,160},{160,192},{192,224},{1,3... | collective-permute-start | bytes 1572872 | tf_op jit(solution)/shard_map/while/body/eval_jaxpr/ppermute | solution.py:29
  386.9 11.4 collective-permute-start
  388.8 9.5 collective-permute-start.1
  425.5 11.0 collective-permute-start
  443.1 11.4 collective-permute-start.2
  456.0 11.4 collective-permute-start
  458.0 9.5 collective-permute-start.1
  468.4 27.8 %collective-permute-start.2 = (bf16[128,2048]{1,0:T(8,128)(2,1)}, bf16[128,2048]{1,0:T(8,128)(2,1)S(1)}, u32[]{:S(2)}, u32[]{:S(2)}) collective-permute-start(bf16[128,2048]{1,0:T(8,128)(2,1)} %get-tuple-element.1251), channel_id=1, source_target_pairs={{0,32},{32,64},{64,96},{96,128},{128,160},{160,192},{192,224},{1,3... | collective-permute-start | bytes 1572872 | tf_op jit(solution)/shard_map/while/body/eval_jaxpr/ppermute | solution.py:29
  497.7 11.4 collective-permute-start
  499.6 9.5 collective-permute-start.1
  510.1 11.4 collective-permute-start.2
  523.0 11.4 collective-permute-start
  525.0 9.5 collective-permute-start.1
  535.4 14.8 %collective-permute-start.2 = (bf16[128,2048]{1,0:T(8,128)(2,1)}, bf16[128,2048]{1,0:T(8,128)(2,1)S(1)}, u32[]{:S(2)}, u32[]{:S(2)}) collective-permute-start(bf16[128,2048]{1,0:T(8,128)(2,1)} %get-tuple-element.1251), channel_id=1, source_target_pairs={{0,32},{32,64},{64,96},{96,128},{128,160},{160,192},{192,224},{1,3... | collective-permute-start | bytes 1572872 | tf_op jit(solution)/shard_map/while/body/eval_jaxpr/ppermute | solution.py:29
  551.8 11.4 collective-permute-start
  553.7 9.5 collective-permute-start.1
  564.2 11.4 collective-permute-start.2
  577.1 11.4 collective-permute-start
  579.1 9.5 collective-permute-start.1
  589.5 24.3 %collective-permute-start.2 = (bf16[128,2048]{1,0:T(8,128)(2,1)}, bf16[128,2048]{1,0:T(8,128)(2,1)S(1)}, u32[]{:S(2)}, u32[]{:S(2)}) collective-permute-start(bf16[128,2048]{1,0:T(8,128)(2,1)} %get-tuple-element.1251), channel_id=1, source_target_pairs={{0,32},{32,64},{64,96},{96,128},{128,160},{160,192},{192,224},{1,3... | collective-permute-start | bytes 1572872 | tf_op jit(solution)/shard_map/while/body/eval_jaxpr/ppermute | solution.py:29
  615.3 11.4 collective-permute-start
  617.2 9.5 collective-permute-start.1
  627.7 11.4 collective-permute-start.2
  642.1 9.7 collective-permute-start.3
  644.1 9.3 collective-permute-start.4
  655.5 9.0 collective-permute-start.5
  673.8 17.1 %collective-permute-start.7 = (bf16[128,2048]{1,0:T(8,128)(2,1)S(1)}, bf16[128,2048]{1,0:T(8,128)(2,1)S(1)}, u32[]{:S(2)}, u32[]{:S(2)}) collective-permute-start(bf16[128,2048]{1,0:T(8,128)(2,1)S(1)} %get-tuple-element.1276), channel_id=1, source_target_pairs={{32,0},{64,32},{96,64},{128,96},{160,128},{192,160},{224,192},{33,... | collective-permute-start | bytes 1572872 | tf_op jit(solution)/shard_map/while/body/eval_jaxpr/ppermute | solution.py:29
  694.8 9.6 collective-permute-start.4
  706.5 9.1 collective-permute-start.5
  724.9 11.3 collective-permute-start.7
  769.1 24.6 %collective-permute-start.7 = (bf16[128,2048]{1,0:T(8,128)(2,1)S(1)}, bf16[128,2048]{1,0:T(8,128)(2,1)S(1)}, u32[]{:S(2)}, u32[]{:S(2)}) collective-permute-start(bf16[128,2048]{1,0:T(8,128)(2,1)S(1)} %get-tuple-element.1276), channel_id=1, source_target_pairs={{32,0},{64,32},{96,64},{128,96},{160,128},{192,160},{224,192},{33,... | collective-permute-start | bytes 1572872 | tf_op jit(solution)/shard_map/while/body/eval_jaxpr/ppermute | solution.py:29
  795.6 9.6 collective-permute-start.3
  808.2 9.0 collective-permute-start.5
  826.5 11.2 collective-permute-start.7
  852.2 9.0 collective-permute-start.5
  870.6 16.0 %collective-permute-start.7 = (bf16[128,2048]{1,0:T(8,128)(2,1)S(1)}, bf16[128,2048]{1,0:T(8,128)(2,1)S(1)}, u32[]{:S(2)}, u32[]{:S(2)}) collective-permute-start(bf16[128,2048]{1,0:T(8,128)(2,1)S(1)} %get-tuple-element.1276), channel_id=1, source_target_pairs={{32,0},{64,32},{96,64},{128,96},{160,128},{192,160},{224,192},{33,... | collective-permute-start | bytes 1572872 | tf_op jit(solution)/shard_map/while/body/eval_jaxpr/ppermute | solution.py:29
  890.4 9.2 collective-permute-start.4
  901.7 9.4 collective-permute-start.5
  920.3 178.7 %collective-permute-start.7 = (bf16[128,2048]{1,0:T(8,128)(2,1)S(1)}, bf16[128,2048]{1,0:T(8,128)(2,1)S(1)}, u32[]{:S(2)}, u32[]{:S(2)}) collective-permute-start(bf16[128,2048]{1,0:T(8,128)(2,1)S(1)} %get-tuple-element.1276), channel_id=1, source_target_pairs={{32,0},{64,32},{96,64},{128,96},{160,128},{192,160},{224,192},{33,... | collective-permute-start | bytes 1572872 | tf_op jit(solution)/shard_map/while/body/eval_jaxpr/ppermute | solution.py:29
  1161.5 11.5 collective-permute-start.7
  1235.4 10.5 collective-permute-start.7
  1260.4 9.0 collective-permute-start.5
  1278.8 29.2 %collective-permute-start.7 = (bf16[128,2048]{1,0:T(8,128)(2,1)S(1)}, bf16[128,2048]{1,0:T(8,128)(2,1)S(1)}, u32[]{:S(2)}, u32[]{:S(2)}) collective-permute-start(bf16[128,2048]{1,0:T(8,128)(2,1)S(1)} %get-tuple-element.1276), channel_id=1, source_target_pairs={{32,0},{64,32},{96,64},{128,96},{160,128},{192,160},{224,192},{33,... | collective-permute-start | bytes 1572872 | tf_op jit(solution)/shard_map/while/body/eval_jaxpr/ppermute | solution.py:29
  (78 other events, 334.3 us)
Sparse Core Ops, SparseCore 0:
  10.6 78.3 all-gather.8
  91.5 79.1 all-gather.10
  173.3 79.1 all-gather.12
  254.9 79.1 all-gather.14
where the time goes:
time: 1320 us
  waiting for transfers between devices  710 us (54%)
  starting transfers between devices  363 us (28%)
  other arithmetic  89.5 us (7%)
  local copies, waits for them, and re-layouts  75.9 us (6%)
  matrix products  59.4 us (4%)
  between operations  13.8 us (1%)
    ppermute x18, waiting for transfers between devices, shifted(): return lax.ppermute(block, axis, route)  301 us
    ppermute x27, starting transfers between devices, padded(): lax.ppermute(lax.slice_in_dim(block, block.shape[dim] - width, None, axis...  191 us
    ppermute x18, starting transfers between devices, shifted(): return lax.ppermute(block, axis, route)  120 us
    select_n x45, other arithmetic, put_slot(): jnp.where(active, lax.dynamic_update_index_in_dim(buffer, value, slot, 0)...  83.1 us
    all_gather x1, waiting for transfers between devices, per_device(): lax.all_gather(w_value[0], 'ctx', axis=0, tiled=True)  81.8 us
    all_gather x1, waiting for transfers between devices, per_device(): lax.all_gather(w_key[0], 'ctx', axis=0, tiled=True)  81.8 us
    all_gather x1, waiting for transfers between devices, per_device(): lax.all_gather(w_out[0], 'ctx', axis=0, tiled=True)  81.6 us
    all_gather x1, waiting for transfers between devices, per_device(): lax.all_gather(w_query[0], 'ctx', axis=0, tiled=True)  78 us
  transfers between devices with their start and end apart: 76, of which 49 were waited for; matrix products, arithmetic and copies ran while one was open for 4% of the time, Pallas kernels for 0%

commit v1 on v0

--- a/solution.py
+++ b/solution.py
@@ -8,6 +8,14 @@
 HDIM = 128
 BLOCKS_DEV = 4
 BLK = 32
+
+
+def gather_from_all(value, axis, dim):
+    devices = lax.axis_size(axis)
+    repeats = [devices if d == dim else 1 for d in range(value.ndim)]
+    return lax.all_to_all(
+        jnp.tile(value, repeats), axis, split_axis=dim, concat_axis=dim, tiled=True
+    )
 
 
 def padded(block, sides, width):
@@ -98,7 +106,7 @@
     length = section_input.shape[1]
     width = HEADS * HDIM
     full_query, full_key, full_value, full_out = (
-        lax.all_gather(w_query[0], "ctx", axis=0, tiled=True),
+        gather_from_all(w_query[0], "ctx", 0),
         lax.all_gather(w_key[0], "ctx", axis=0, tiled=True),
         lax.all_gather(w_value[0], "ctx", axis=0, tiled=True),
         lax.all_gather(w_out[0], "ctx", axis=0, tiled=True),

time: 1320 us -> 1300 us (0.985)
  waiting for transfers between devices: 710 us -> 691 us
    all_to_all x0 -> x1, waiting for transfers between devices: none -> 116 us  [gather_from_all(): lax.all_to_all(jnp.tile(value, repeats), axis, split_axis=dim, concat_axi...]
    all_gather x1, waiting for transfers between devices: 81.8 us -> 2.87 us  [per_device(): lax.all_gather(w_key[0], 'ctx', axis=0, tiled=True)]
    all_gather x1 -> x0, waiting for transfers between devices: 78 us -> none  [per_device(): lax.all_gather(w_query[0], 'ctx', axis=0, tiled=True)]
    ppermute x18, waiting for transfers between devices: 301 us -> 328 us  [shifted(): return lax.ppermute(block, axis, route)]
    while x54, local copies, waits for them, and re-layouts: 14.1 us -> 0.48 us
  transfers between devices with their start and end apart: 76 -> 76, of which waited for: 49 -> 49; matrix products, arithmetic and copies ran while one was open for 4% -> 3% of each run, Pallas kernels for 0% -> 0%
where the time goes in v1:
time: 1300 us
  waiting for transfers between devices  691 us (53%)
  starting transfers between devices  376 us (29%)
  other arithmetic  81.4 us (6%)
  local copies, waits for them, and re-layouts  72.8 us (6%)
  matrix products  59.4 us (5%)
  between operations  13.8 us (1%)
    ppermute x18, waiting for transfers between devices, shifted(): return lax.ppermute(block, axis, route)  328 us
    ppermute x27, starting transfers between devices, padded(): lax.ppermute(lax.slice_in_dim(block, block.shape[dim] - width, None, axis...  191 us
    ppermute x18, starting transfers between devices, shifted(): return lax.ppermute(block, axis, route)  123 us
    all_to_all x1, waiting for transfers between devices, gather_from_all(): lax.all_to_all(jnp.tile(value, repeats), axis, split_axis=dim, concat_axi...  116 us
    all_gather x1, waiting for transfers between devices, per_device(): lax.all_gather(w_out[0], 'ctx', axis=0, tiled=True)  81.8 us
    all_gather x1, waiting for transfers between devices, per_device(): lax.all_gather(w_value[0], 'ctx', axis=0, tiled=True)  78 us
    select_n x45, other arithmetic, put_slot(): jnp.where(active, lax.dynamic_update_index_in_dim(buffer, value, slot, 0)...  71.4 us
    ppermute x27, waiting for transfers between devices, padded(): lax.ppermute(lax.slice_in_dim(block, 0, width, axis=dim), axis, backward)  69 us
  transfers between devices with their start and end apart: 76, of which 49 were waited for; matrix products, arithmetic and copies ran while one was open for 3% of the time, Pallas kernels for 0%

profile of v1, /device:TPU:103, one launch (start us, length us, event | category | flops | bytes accessed | tf_op | source)
XLA Modules:
  0.0 1298.4 jit_solution(17566061720862439847)
XLA Ops:
  12.0 9.8 all-to-all-start
  23.0 115.7 %all-to-all-done = bf16[32,64,1024]{2,1,0:T(8,128)(2,1)} async-done(((bf16[32,64,1024]{2,1,0:T(8,128)(2,1)}), bf16[32,64,1024]{2,1,0:T(8,128)(2,1)}, u32[]{:S(2)}, u32[]{:S(2)}) %all-to-all-start) | async-done | bytes 4194336 | tf_op jit(solution)/shard_map/all_to_all | solution.py:16
  141.5 78.0 %all-gather.9.cloned.1.call-done = bf16[1,2048,1024]{2,1,0:T(8,128)(2,1)} async-done(((bf16[1,64,1024]{2,1,0:T(8,128)(2,1)}), bf16[1,2048,1024]{2,1,0:T(8,128)(2,1)}) %all-gather.9.cloned.1.call-update) | async-done | bytes 4194320 | tf_op jit(solution)/shard_map/all_gather | solution.py:111
  219.5 81.8 %all-gather.11.cloned.1.call-done = bf16[1,1024,2048]{2,1,0:T(8,128)(2,1)} async-done(((bf16[1,32,2048]{2,1,0:T(8,128)(2,1)}), bf16[1,1024,2048]{2,1,0:T(8,128)(2,1)}) %all-gather.11.cloned.1.call-update) | async-done | bytes 4194320 | tf_op jit(solution)/shard_map/all_gather | solution.py:112
  305.4 306.8 %while.41 = (s32[]{:T(128)}, bf16[128,2048]{1,0:T(8,128)(2,1)}, bf16[2,128,2048]{2,1,0:T(8,128)(2,1)S(1)}, bf16[2,128,2048]{2,1,0:T(8,128)(2,1)}, bf16[2,128,102...) while((s32[]{:T(128)}, bf16[128,2048]{1,0:T(8,128)(2,1)}, ...), condition=%wide.region_9.10_spmd, body=%wide.region_0.9_spmd.sunk | while | flops 2211841024 | bytes 80431864 | solution.py:159
  318.7 7.9 collective-permute-start.2
  328.9 14.7 %collective-permute-done.2 = bf16[128,2048]{1,0:T(8,128)(2,1)} collective-permute-done((bf16[128,2048]{1,0:T(8,128)(2,1)}, bf16[128,2048]{1,0:T(8,128)(2,1)}, u32[]{:S(2)}, u32[]{:S(2)}) %collective-permute-start.2) | collective-permute-done | bytes 524320 | tf_op jit(solution)/shard_map/while/body/eval_jaxpr/ppermute | solution.py:37
  345.0 10.8 conditional.8
  357.9 7.4 collective-permute-start.1
  367.4 7.3 conditional.9
  384.5 10.9 conditional.8
  406.5 7.3 conditional.9
  428.9 7.4 collective-permute-start.1
  439.4 22.2 %collective-permute-start.2 = (bf16[128,2048]{1,0:T(8,128)(2,1)}, bf16[128,2048]{1,0:T(8,128)(2,1)}, u32[]{:S(2)}, u32[]{:S(2)}) collective-permute-start(bf16[128,2048]{1,0:T(8,128)(2,1)} %get-tuple-element.1251), channel_id=1, source_target_pairs={{0,32},{32,64},{64,96},{96,128},{128,160},{160,192},{192,224},{1,3... | collective-permute-start | bytes 1572872 | tf_op jit(solution)/shard_map/while/body/eval_jaxpr/ppermute | solution.py:37
  471.6 7.4 collective-permute-start.1
  497.2 7.4 collective-permute-start.1
  507.7 7.8 collective-permute-start.2
  525.5 7.4 collective-permute-start.1
  551.1 7.4 collective-permute-start.1
  561.6 18.6 %collective-permute-start.2 = (bf16[128,2048]{1,0:T(8,128)(2,1)}, bf16[128,2048]{1,0:T(8,128)(2,1)}, u32[]{:S(2)}, u32[]{:S(2)}) collective-permute-start(bf16[128,2048]{1,0:T(8,128)(2,1)} %get-tuple-element.1251), channel_id=1, source_target_pairs={{0,32},{32,64},{64,96},{96,128},{128,160},{160,192},{192,224},{1,3... | collective-permute-start | bytes 1572872 | tf_op jit(solution)/shard_map/while/body/eval_jaxpr/ppermute | solution.py:37
  590.2 7.4 collective-permute-start.1
  613.3 678.6 %while.42 = (s32[]{:T(128)}, bf16[128,2048]{1,0:T(8,128)(2,1)S(1)}, bf16[2,128,2048]{2,1,0:T(8,128)(2,1)}, s32[]{:T(128)}, bf16[2,2,128,1024]{3,2,1,0:T(8,128)(2...) while((s32[]{:T(128)}, bf16[128,2048]{1,0:T(8,128)(2,1)S(1)}, ...), condition=%wide.region_24.25_spmd, body=%wide.region_10.24_spmd.sunk | while | flops 3389073152 | bytes 162784752 | solution.py:206
  616.4 7.4 collective-permute-start.4
  636.8 7.2 collective-permute-done.6
  648.2 14.5 %collective-permute-done.7 = bf16[128,2048]{1,0:T(8,128)(2,1)S(1)} collective-permute-done((bf16[128,2048]{1,0:T(8,128)(2,1)S(1)}, bf16[128,2048]{1,0:T(8,128)(2,1)S(1)}, u32[]{:S(2)}, u32[]{:S(2)}) %collective-permute-start.7) | collective-permute-done | bytes 524320 | tf_op jit(solution)/shard_map/while/body/eval_jaxpr/ppermute | solution.py:37
  677.6 7.5 collective-permute-start.5
  687.0 7.2 collective-permute-done.6
  698.4 8.6 collective-permute-done.7
  729.7 7.2 collective-permute-done.6
  741.1 24.7 %collective-permute-done.7 = bf16[128,2048]{1,0:T(8,128)(2,1)S(1)} collective-permute-done((bf16[128,2048]{1,0:T(8,128)(2,1)S(1)}, bf16[128,2048]{1,0:T(8,128)(2,1)S(1)}, u32[]{:S(2)}, u32[]{:S(2)}) %collective-permute-start.7) | collective-permute-done | bytes 524320 | tf_op jit(solution)/shard_map/while/body/eval_jaxpr/ppermute | solution.py:37
  788.5 7.2 collective-permute-done.6
  799.9 9.5 collective-permute-done.7
  832.2 7.2 collective-permute-done.6
  843.5 16.6 %collective-permute-done.7 = bf16[128,2048]{1,0:T(8,128)(2,1)S(1)} collective-permute-done((bf16[128,2048]{1,0:T(8,128)(2,1)S(1)}, bf16[128,2048]{1,0:T(8,128)(2,1)S(1)}, u32[]{:S(2)}, u32[]{:S(2)}) %collective-permute-start.7) | collective-permute-done | bytes 524320 | tf_op jit(solution)/shard_map/while/body/eval_jaxpr/ppermute | solution.py:37
  882.9 7.2 collective-permute-done.6
  894.2 186.3 %collective-permute-done.7 = bf16[128,2048]{1,0:T(8,128)(2,1)S(1)} collective-permute-done((bf16[128,2048]{1,0:T(8,128)(2,1)S(1)}, bf16[128,2048]{1,0:T(8,128)(2,1)S(1)}, u32[]{:S(2)}, u32[]{:S(2)}) %collective-permute-start.7) | collective-permute-done | bytes 524320 | tf_op jit(solution)/shard_map/while/body/eval_jaxpr/ppermute | solution.py:37
  1092.2 11.7 conditional.10
  1105.1 7.1 collective-permute-start.5
  1114.1 7.2 collective-permute-done.6
  1121.3 20.3 %conditional.11 = (bf16[128,2048]{1,0:T(8,128)(2,1)S(1)}) conditional(s32[]{:T(128)} %convert_element_type.302, () %tuple.209, (bf16[2,192,1024]{2,1,0:T(8,128)(2,1)S(1)}, bf16[2,32,1024]{2,1,0:T(8,128)(2,1)}, bf16[2,32,1024]{2,1,0:T(8,128)(2,1)}, bf16[2048,1024]{1,0:T(8,128)(2,1)}, bf16[2,128,2048]{2,1,0:T(8,128)(2,1)S(1)}, /*index=5*/s32[]{:T(128)}, ...), branch_computations={%region_15.15_spmd, %region_16.23_spmd} | conditional | flops 2693800704 | bytes 88217256 | solution.py:200
  1145.7 9.5 collective-permute-done.7
  1167.0 11.7 conditional.10
  1179.8 7.1 collective-permute-start.5
  1188.8 7.2 collective-permute-done.6
  1196.0 20.3 %conditional.11 = (bf16[128,2048]{1,0:T(8,128)(2,1)S(1)}) conditional(s32[]{:T(128)} %convert_element_type.302, () %tuple.209, (bf16[2,192,1024]{2,1,0:T(8,128)(2,1)S(1)}, bf16[2,32,1024]{2,1,0:T(8,128)(2,1)}, bf16[2,32,1024]{2,1,0:T(8,128)(2,1)}, bf16[2048,1024]{1,0:T(8,128)(2,1)}, bf16[2,128,2048]{2,1,0:T(8,128)(2,1)S(1)}, /*index=5*/s32[]{:T(128)}, ...), branch_computations={%region_15.15_spmd, %region_16.23_spmd} | conditional | flops 2693800704 | bytes 88217256 | solution.py:200
  1220.5 8.6 collective-permute-done.7
  1251.8 7.2 collective-permute-done.6
  1261.2 29.1 %collective-permute-start.7 = (bf16[128,2048]{1,0:T(8,128)(2,1)S(1)}, bf16[128,2048]{1,0:T(8,128)(2,1)S(1)}, u32[]{:S(2)}, u32[]{:S(2)}) collective-permute-start(bf16[128,2048]{1,0:T(8,128)(2,1)S(1)} %get-tuple-element.1276), channel_id=1, source_target_pairs={{32,0},{64,32},{96,64},{128,96},{160,128},{192,160},{224,192},{33,... | collective-permute-start | bytes 1572872 | tf_op jit(solution)/shard_map/while/body/eval_jaxpr/ppermute | solution.py:37
  (682 shorter events, 485.1 us)
Async XLA Ops:
  7.2 134.3 %all-gather.7.cloned.1.call-start = ((), (), s32[]{:S(2)}) async-start(), calls=%async_computation.1 | async-start | bytes 4325376 | tf_op jit(solution)/shard_map/all_gather | solution.py:110
  7.9 211.6 %all-gather.9.cloned.1.call-start = ((), (), s32[]{:S(2)}) async-start(), calls=%async_computation.2 | async-start | bytes 4325376 | tf_op jit(solution)/shard_map/all_gather | solution.py:111
  12.0 126.6 %all-to-all-start = ((bf16[32,64,1024]{2,1,0:T(8,128)(2,1)}), bf16[32,64,1024]{2,1,0:T(8,128)(2,1)}, u32[]{:S(2)}, u32[]{:S(2)}) async-start(bf16[32,64,1024]{2,1,0:T(8,128)(2,1)} %tile.9), calls=%async_computation | async-start | bytes 8388608 | tf_op jit(solution)/shard_map/all_to_all | solution.py:16
  21.9 279.4 %all-gather.11.cloned.1.call-start = ((), (), s32[]{:S(2)}) async-start(), calls=%async_computation.3 | async-start | bytes 4325376 | tf_op jit(solution)/shard_map/all_gather | solution.py:112
  307.0 10.7 collective-permute-start
  318.7 24.8 %collective-permute-start.2 = (bf16[128,2048]{1,0:T(8,128)(2,1)}, bf16[128,2048]{1,0:T(8,128)(2,1)}, u32[]{:S(2)}, u32[]{:S(2)}) collective-permute-start(bf16[128,2048]{1,0:T(8,128)(2,1)} %get-tuple-element.1251), channel_id=1, source_target_pairs={{0,32},{32,64},{64,96},{96,128},{128,160},{160,192},{192,224},{1,3... | collective-permute-start | bytes 1572872 | tf_op jit(solution)/shard_map/while/body/eval_jaxpr/ppermute | solution.py:37
  356.0 11.4 collective-permute-start
  357.9 9.4 collective-permute-start.1
  395.5 10.9 collective-permute-start
  413.8 11.5 collective-permute-start.2
  427.0 11.4 collective-permute-start
  428.9 9.5 collective-permute-start.1
  439.4 28.6 %collective-permute-start.2 = (bf16[128,2048]{1,0:T(8,128)(2,1)}, bf16[128,2048]{1,0:T(8,128)(2,1)}, u32[]{:S(2)}, u32[]{:S(2)}) collective-permute-start(bf16[128,2048]{1,0:T(8,128)(2,1)} %get-tuple-element.1251), channel_id=1, source_target_pairs={{0,32},{32,64},{64,96},{96,128},{128,160},{160,192},{192,224},{1,3... | collective-permute-start | bytes 1572872 | tf_op jit(solution)/shard_map/while/body/eval_jaxpr/ppermute | solution.py:37
  469.7 11.4 collective-permute-start
  471.6 9.5 collective-permute-start.1
  482.1 11.5 collective-permute-start.2
  495.3 11.4 collective-permute-start
  497.2 9.5 collective-permute-start.1
  507.7 14.2 %collective-permute-start.2 = (bf16[128,2048]{1,0:T(8,128)(2,1)}, bf16[128,2048]{1,0:T(8,128)(2,1)}, u32[]{:S(2)}, u32[]{:S(2)}) collective-permute-start(bf16[128,2048]{1,0:T(8,128)(2,1)} %get-tuple-element.1251), channel_id=1, source_target_pairs={{0,32},{32,64},{64,96},{96,128},{128,160},{160,192},{192,224},{1,3... | collective-permute-start | bytes 1572872 | tf_op jit(solution)/shard_map/while/body/eval_jaxpr/ppermute | solution.py:37
  523.6 11.4 collective-permute-start
  525.5 9.5 collective-permute-start.1
  536.0 11.5 collective-permute-start.2
  549.2 11.4 collective-permute-start
  551.1 9.5 collective-permute-start.1
  561.6 25.0 %collective-permute-start.2 = (bf16[128,2048]{1,0:T(8,128)(2,1)}, bf16[128,2048]{1,0:T(8,128)(2,1)}, u32[]{:S(2)}, u32[]{:S(2)}) collective-permute-start(bf16[128,2048]{1,0:T(8,128)(2,1)} %get-tuple-element.1251), channel_id=1, source_target_pairs={{0,32},{32,64},{64,96},{96,128},{128,160},{160,192},{192,224},{1,3... | collective-permute-start | bytes 1572872 | tf_op jit(solution)/shard_map/while/body/eval_jaxpr/ppermute | solution.py:37
  588.3 11.4 collective-permute-start
  590.2 9.5 collective-permute-start.1
  600.6 11.5 collective-permute-start.2
  614.4 9.7 collective-permute-start.3
  616.4 9.3 collective-permute-start.4
  634.9 9.1 collective-permute-start.6
  646.2 16.5 %collective-permute-start.7 = (bf16[128,2048]{1,0:T(8,128)(2,1)S(1)}, bf16[128,2048]{1,0:T(8,128)(2,1)S(1)}, u32[]{:S(2)}, u32[]{:S(2)}) collective-permute-start(bf16[128,2048]{1,0:T(8,128)(2,1)S(1)} %get-tuple-element.1276), channel_id=1, source_target_pairs={{32,0},{64,32},{96,64},{128,96},{160,128},{192,160},{224,192},{33,... | collective-permute-start | bytes 1572872 | tf_op jit(solution)/shard_map/while/body/eval_jaxpr/ppermute | solution.py:37
  665.7 9.7 collective-permute-start.4
  677.6 9.5 collective-permute-start.5
  685.1 9.1 collective-permute-start.6
  696.5 10.5 collective-permute-start.7
  727.8 9.1 collective-permute-start.6
  739.1 26.6 %collective-permute-start.7 = (bf16[128,2048]{1,0:T(8,128)(2,1)S(1)}, bf16[128,2048]{1,0:T(8,128)(2,1)S(1)}, u32[]{:S(2)}, u32[]{:S(2)}) collective-permute-start(bf16[128,2048]{1,0:T(8,128)(2,1)S(1)} %get-tuple-element.1276), channel_id=1, source_target_pairs={{32,0},{64,32},{96,64},{128,96},{160,128},{192,160},{224,192},{33,... | collective-permute-start | bytes 1572872 | tf_op jit(solution)/shard_map/while/body/eval_jaxpr/ppermute | solution.py:37
  766.9 9.5 collective-permute-start.3
  786.6 9.1 collective-permute-start.6
  797.9 11.5 collective-permute-start.7
  830.2 9.1 collective-permute-start.6
  841.6 18.5 %collective-permute-start.7 = (bf16[128,2048]{1,0:T(8,128)(2,1)S(1)}, bf16[128,2048]{1,0:T(8,128)(2,1)S(1)}, u32[]{:S(2)}, u32[]{:S(2)}) collective-permute-start(bf16[128,2048]{1,0:T(8,128)(2,1)S(1)} %get-tuple-element.1276), channel_id=1, source_target_pairs={{32,0},{64,32},{96,64},{128,96},{160,128},{192,160},{224,192},{33,... | collective-permute-start | bytes 1572872 | tf_op jit(solution)/shard_map/while/body/eval_jaxpr/ppermute | solution.py:37
  892.3 188.2 %collective-permute-start.7 = (bf16[128,2048]{1,0:T(8,128)(2,1)S(1)}, bf16[128,2048]{1,0:T(8,128)(2,1)S(1)}, u32[]{:S(2)}, u32[]{:S(2)}) collective-permute-start(bf16[128,2048]{1,0:T(8,128)(2,1)S(1)} %get-tuple-element.1276), channel_id=1, source_target_pairs={{32,0},{64,32},{96,64},{128,96},{160,128},{192,160},{224,192},{33,... | collective-permute-start | bytes 1572872 | tf_op jit(solution)/shard_map/while/body/eval_jaxpr/ppermute | solution.py:37
  1143.8 11.4 collective-permute-start.7
  1218.5 10.5 collective-permute-start.7
  1249.9 9.1 collective-permute-start.6
  1261.2 30.7 %collective-permute-start.7 = (bf16[128,2048]{1,0:T(8,128)(2,1)S(1)}, bf16[128,2048]{1,0:T(8,128)(2,1)S(1)}, u32[]{:S(2)}, u32[]{:S(2)}) collective-permute-start(bf16[128,2048]{1,0:T(8,128)(2,1)S(1)} %get-tuple-element.1276), channel_id=1, source_target_pairs={{32,0},{64,32},{96,64},{128,96},{160,128},{192,160},{224,192},{33,... | collective-permute-start | bytes 1572872 | tf_op jit(solution)/shard_map/while/body/eval_jaxpr/ppermute | solution.py:37
  (71 other events, 489.4 us)
Sparse Core Ops, SparseCore 0:
  10.6 130.8 all-gather.6
  144.1 75.3 all-gather.8
  222.1 79.1 all-gather.10
